TPU v7x, 128 devices: a whole 4x4x4 slice. The times are simulated.
128 devices in a mesh: grp: 4 (over x_hi, core), dom: 32 (over z, y, x_lo).
Axes of the slice: x: 4 (x_hi: 2, x_lo: 2; x = x_hi * 2 + x_lo), y: 4, z: 4, core: 2. Of those that a mesh axis runs over, the one named last changes fastest.
Arguments:
- nodes: bfloat16 [131072, 256], P(('grp', 'dom')), may hold values from -8 to 8
- neighbours: int32 [131072, 8], P(('grp', 'dom')), may hold values from 0 to 1279
- send_rows: int32 [32768], P(('grp', 'dom')), may hold values from 0 to 1023
- landmark_ids: int32 [8192], P(('grp', 'dom')), may hold values from 0 to 1023
- w_dst: bfloat16 [256, 256], replicated, may hold values from -0.375 to 0.375
- w_src: bfloat16 [256, 256], replicated, may hold values from -0.375 to 0.375
- w_msg: bfloat16 [256, 256], replicated, may hold values from -0.375 to 0.375
- edge_bias: float32 [256], replicated, may hold values from -4 to 4
- w_query: bfloat16 [256, 256], replicated, may hold values from -0.375 to 0.375
- w_key: bfloat16 [256, 256], replicated, may hold values from -0.375 to 0.375
- w_value: bfloat16 [256, 256], replicated, may hold values from -0.375 to 0.375
- w_out: bfloat16 [256, 256], replicated, may hold values from -0.375 to 0.375
Outputs:
- result: bfloat16 [131072, 256], P(('grp', 'dom'))
- kernel_term: float32 [131072, 256], P(('grp', 'dom'))
Inputs may be any that keep to these rules, and one draw needn't show every extreme that they name: `neighbours`: entries index the device's own 1024 rows, then the 128 rows received from the previous partition, then the 128 rows from the next one. `send_rows`: each partition's entries are rows of its own nodes. `landmark_ids`: each partition's entries are rows of its own nodes.
All inputs are finite; a program needn't handle non-finite values.
Results may differ from a plain program's by a relative error of at most 0.0054.
Values may be sent and summed in bfloat16 or wider, within the bound.
A program may use at most 64 MiB of HBM per device.

v0:
```python
import math

import jax
import jax.numpy as jnp
from jax import lax
from jax.sharding import PartitionSpec as P


def extended_2(cells, sides, width):
    for axis, dim in sides:
        count = lax.axis_size(axis)
        head = lax.slice_in_dim(cells, 0, width, axis=dim)
        tail = lax.slice_in_dim(cells, cells.shape[dim] - width, cells.shape[dim], axis=dim)
        cells = jnp.concatenate(
            [
                lax.ppermute(tail, axis, [(i, (i + 1) % count) for i in range(count)]),
                cells,
                lax.ppermute(head, axis, [((i + 1) % count, i) for i in range(count)]),
            ],
            axis=dim,
        )
    return cells


def rms_scale(values):
    return values * lax.rsqrt(jnp.mean(values * values, axis=-1, keepdims=True) + 1e-06)


def kernel_tile(query, key_rows):
    scale = 2.0 * query.shape[1] ** (-0.5)
    return jnp.exp(jnp.dot(query, key_rows.T, preferred_element_type=jnp.float32) * scale).astype(
        jnp.bfloat16
    )


def partial_sums(query, value, key_rows):
    total_rows = key_rows.shape[0]
    block_size = math.gcd(total_rows, 512)
    blocks = key_rows.reshape(total_rows // block_size, block_size, key_rows.shape[1])

    def partial_one_block(block_keys):
        kernel = kernel_tile(query, block_keys)
        return lax.dot_general(
            kernel, value, (((0,), (0,)), ((), ())), preferred_element_type=jnp.float32
        )

    return lax.map(partial_one_block, blocks).reshape(total_rows, value.shape[1])


def apply_sums(query, key_rows, sum_rows):
    total_rows = key_rows.shape[0]
    block_size = math.gcd(total_rows, 512)
    key_blocks = key_rows.reshape(total_rows // block_size, block_size, key_rows.shape[1])
    sum_blocks = sum_rows.reshape(total_rows // block_size, block_size, sum_rows.shape[1])

    def apply_one_block(accum, pair):
        block_keys, block_sums = pair
        kernel = kernel_tile(query, block_keys)
        return (accum + jnp.dot(kernel, block_sums, preferred_element_type=jnp.float32), None)

    start_value = jnp.zeros((query.shape[0], sum_rows.shape[1]), jnp.float32)
    accum, _ = lax.scan(apply_one_block, start_value, (key_blocks, sum_blocks))
    return accum


def shards(
    nodes,
    neighbours,
    send_rows,
    landmark_ids,
    w_dst,
    w_src,
    w_msg,
    edge_bias,
    w_query,
    w_key,
    w_value,
    w_out,
):
    halo_count = send_rows.shape[0] // 2
    outgoing = jnp.concatenate(
        [nodes[send_rows[:halo_count]], nodes[send_rows[halo_count:]]], axis=0
    )
    padded = extended_2(outgoing, ((("grp", "dom"), 0),), halo_count)
    extended = jnp.concatenate([nodes, padded[:halo_count], padded[3 * halo_count :]], axis=0)
    source = jnp.dot(extended, w_src, preferred_element_type=jnp.float32)
    target = jnp.dot(nodes, w_dst, preferred_element_type=jnp.float32)
    preact = target[:, None, :] + source[neighbours] + edge_bias
    messages = jnp.mean(jax.nn.gelu(preact), axis=1).astype(jnp.bfloat16)
    updated = (
        nodes.astype(jnp.float32) + jnp.dot(messages, w_msg, preferred_element_type=jnp.float32)
    ).astype(jnp.bfloat16)
    normed = rms_scale(updated.astype(jnp.float32)).astype(jnp.bfloat16)
    query = jnp.dot(normed, w_query, preferred_element_type=jnp.float32).astype(jnp.bfloat16)
    value = jnp.dot(normed, w_value, preferred_element_type=jnp.float32).astype(jnp.bfloat16)
    local_keys = jnp.dot(normed[landmark_ids], w_key, preferred_element_type=jnp.float32).astype(
        jnp.bfloat16
    )
    all_keys = lax.all_gather(local_keys, ("grp", "dom"), axis=0, tiled=True)
    own_sums = partial_sums(query, value, all_keys)
    total_sums = lax.psum(own_sums, ("grp", "dom")).astype(jnp.bfloat16)
    smooth = apply_sums(query, all_keys, total_sums)
    kernel_term = rms_scale(smooth)
    scaled = kernel_term.astype(jnp.bfloat16)
    result = updated.astype(jnp.float32) + jnp.dot(
        scaled, w_out, preferred_element_type=jnp.float32
    )
    return (result.astype(jnp.bfloat16), kernel_term)


def solution(mesh):
    return jax.shard_map(
        shards,
        mesh=mesh,
        in_specs=(
            P(("grp", "dom"), None),
            P(("grp", "dom"), None),
            P(("grp", "dom")),
            P(("grp", "dom")),
            P(),
            P(),
            P(),
            P(),
            P(),
            P(),
            P(),
            P(),
        ),
        out_specs=(P(("grp", "dom"), None), P(("grp", "dom"), None)),
        check_vma=False,
    )
```

profile of v0, /device:TPU:0, one launch (start us, length us, event | category | flops | bytes accessed | tf_op | source)
XLA Modules:
  0.0 572.5 jit_solution(5054479233434508780)
XLA Ops:
  8.0 1.9 gather_fusion
  9.9 1.6 collective-permute-start
  11.5 1.9 gather_fusion.1
  13.4 6.7 %collective-permute-start.1 = (bf16[128,256]{1,0:T(8,128)(2,1)S(1)}, bf16[128,256]{1,0:T(8,128)(2,1)}, u32[]{:S(2)}, u32[]{:S(2)}) collective-permute-start(bf16[128,256]{1,0:T(8,128)(2,1)S(1)} %gather_fusion.1), channel_id=1, source_target_pairs={{1,0},{2,1},{3,2},{4,3},{5,4},{6,5},{7,6},{8,7},{9,8},{10,9},{11,1... | collective-permute-start | bytes 196616 | tf_op jit(solution)/shard_map/ppermute | solution.py:18
  20.1 1.2 copy.18
  21.4 0.8 compare_select_fusion
  22.6 1.4 fusion.46
  25.3 1.4 fusion.36
  26.7 31.6 %gather_fusion.2 = f32[8192,256]{1,0:T(8,128)} fusion(f32[1280,256]{1,0:T(8,128)S(1)} %fusion.36, s32[8192]{0:T(1024)S(1)} %broadcast_clamp_fusion), kind=kCustom, calls=%fused_computation.2 | custom fusion | bytes 16809984 | tf_op jit(solution)/shard_map/gather | solution.py:88
  58.3 7.8 %fusion.30 = f32[1024,256]{1,0:T(8,128)S(1)} fusion(f32[8192,256]{1,0:T(8,128)} %gather_fusion.2, f32[256]{0:T(256)S(1)} %copy-done.8, f32[1024,256]{1,0:T(8,128)S(1)} %fusion.46), kind=kLoop, calls=%fused_computation.31 | loop fusion | flops 22806528 | bytes 10486784 | tf_op jit(solution)/shard_map/reduce_sum | solution.py:89
  67.6 0.8 convolution_convert_fusion.2
  69.2 302.4 %all-gather.2.cloned.1.call-done = bf16[8192,256]{1,0:T(8,128)(2,1)} async-done(((bf16[64,256]{1,0:T(8,128)(2,1)}), bf16[8192,256]{1,0:T(8,128)(2,1)}) %all-gather.2.cloned.1.call-update) | async-done | bytes 4194320 | tf_op jit(solution)/shard_map/all_gather | solution.py:99
  371.6 41.7 %while.21 = (s32[]{:T(128)}, f32[16,512,256]{2,1,0:T(8,128)}, bf16[16,512,256]{2,1,0:T(8,128)(2,1)}, bf16[1024,256]{1,0:T(8,128)(2,1)S(1)}, bf16[1024,256]{1,0:T(8,128)(2,1)S(1)}, /*index=5*/s32[]{:T(128)}) while((s32[]{:T(128)}, f32[16,512,256]{2,1,0:T(8,128)}, bf16[16,512,256]{2,1,0:T(8,128)(2,1)}, bf16[1024,256]{1,0:T(8,128)(2,1)S(1)}, ...), condition=%wide.region_3.4_spmd, body=%wide.region_2.3_spmd.sunk | while | flops 537919488 | bytes 1836101 | solution.py:47
  371.6 2.6 fusion.72
  374.2 2.6 fusion.72
  376.8 2.6 fusion.72
  379.4 2.6 fusion.72
  382.0 2.6 fusion.72
  384.6 2.6 fusion.72
  387.2 2.6 fusion.72
  389.8 2.6 fusion.72
  392.4 2.6 fusion.72
  395.0 2.6 fusion.72
  397.6 2.6 fusion.72
  400.2 2.6 fusion.72
  402.8 2.6 fusion.72
  405.4 2.6 fusion.72
  408.0 2.6 fusion.72
  410.6 2.6 fusion.72
  413.3 114.5 %all-reduce.1 = bf16[8192,256]{1,0:T(8,128)(2,1)} all-reduce(f32[8192,256]{1,0:T(8,128)} %bitcast.52), channel_id=1, replica_groups=mesh['grp'=4,'dom'=32] {'grp','dom'}, use_global_device_ids=true, to_apply=%region_4.5 | all-reduce | flops 2097152 | bytes 12582912 | tf_op jit(solution)/shard_map/psum | solution.py:101
  527.7 36.1 %while.22 = (s32[]{:T(128)}, f32[1024,256]{1,0:T(8,128)S(1)}, bf16[16,512,256]{2,1,0:T(8,128)(2,1)}, bf16[1024,256]{1,0:T(8,128)(2,1)S(1)}, bf16[16,512,256]{2,1,0:T(8,128)(2,1)}, /*index=5*/s32[]{:T(128)}, s32[]{:T(128)}) while((s32[]{:T(128)}, f32[1024,256]{1,0:T(8,128)S(1)}, bf16[16,512,256]{2,1,0:T(8,128)(2,1)}, ...), condition=%wide.region_6.7_spmd.clone, body=%wide.region_5.6_spmd.clone.sunk | while | flops 538443776 | bytes 3146839 | solution.py:62
  527.7 2.3 fusion.76
  530.0 2.2 fusion.76
  532.3 2.2 fusion.76
  534.5 2.2 fusion.76
  536.8 2.2 fusion.76
  539.0 2.2 fusion.76
  541.3 2.2 fusion.76
  543.5 2.2 fusion.76
  545.8 2.2 fusion.76
  548.0 2.2 fusion.76
  550.3 2.2 fusion.76
  552.5 2.2 fusion.76
  554.8 2.2 fusion.76
  557.1 2.2 fusion.76
  559.3 2.2 fusion.76
  561.6 2.2 fusion.76
  564.6 1.0 copy.22
  (43 shorter events, 5.5 us)
Async XLA Ops:
  7.2 18.1 %copy-start = (bf16[256,256]{1,0:T(8,128)(2,1)S(1)}, bf16[256,256]{1,0:T(8,128)(2,1)}, u32[]{:S(2)}) copy-start(bf16[256,256]{1,0:T(8,128)(2,1)} %param.21) | copy-start | bytes 393220
  7.2 364.4 %all-gather.2.cloned.1.call-start = ((), (), s32[]{:S(2)}) async-start(), calls=%async_computation | async-start | bytes 4227072 | tf_op jit(solution)/shard_map/all_gather | solution.py:99
  9.9 14.8 %collective-permute-start = (bf16[128,256]{1,0:T(8,128)(2,1)S(1)}, bf16[128,256]{1,0:T(8,128)(2,1)S(1)}, u32[]{:S(2)}, u32[]{:S(2)}) collective-permute-start(bf16[128,256]{1,0:T(8,128)(2,1)S(1)} %gather_fusion), channel_id=1, source_target_pairs={{0,1},{1,2},{2,3},{3,4},{4,5},{5,6},{6,7},{7,8},{8,9},{9,10},{10,1... | collective-permute-start | bytes 196616 | tf_op jit(solution)/shard_map/ppermute | solution.py:16
  13.4 11.9 %collective-permute-start.1 = (bf16[128,256]{1,0:T(8,128)(2,1)S(1)}, bf16[128,256]{1,0:T(8,128)(2,1)}, u32[]{:S(2)}, u32[]{:S(2)}) collective-permute-start(bf16[128,256]{1,0:T(8,128)(2,1)S(1)} %gather_fusion.1), channel_id=1, source_target_pairs={{1,0},{2,1},{3,2},{4,3},{5,4},{6,5},{7,6},{8,7},{9,8},{10,9},{11,1... | collective-permute-start | bytes 196616 | tf_op jit(solution)/shard_map/ppermute | solution.py:18
  24.6 0.6 copy-start.7
  26.7 31.6 %copy-start.8 = (f32[256]{0:T(256)S(1)}, f32[256]{0:T(256)}, u32[]{:S(2)}) copy-start(f32[256]{0:T(256)} %param.23) | copy-start | bytes 3076
  58.3 7.9 %copy-start.2 = (bf16[256,256]{1,0:T(8,128)(2,1)S(1)}, bf16[256,256]{1,0:T(8,128)(2,1)}, u32[]{:S(2)}) copy-start(bf16[256,256]{1,0:T(8,128)(2,1)} %param.22) | copy-start | bytes 393220
  58.3 9.3 %copy-start.6 = (bf16[256,256]{1,0:T(8,128)(2,1)S(1)}, bf16[256,256]{1,0:T(8,128)(2,1)}, u32[]{:S(2)}) copy-start(bf16[256,256]{1,0:T(8,128)(2,1)} %param.25) | copy-start | bytes 393220
  58.3 10.1 %copy-start.3 = (bf16[256,256]{1,0:T(8,128)(2,1)S(1)}, bf16[256,256]{1,0:T(8,128)(2,1)}, u32[]{:S(2)}) copy-start(bf16[256,256]{1,0:T(8,128)(2,1)} %param.24) | copy-start | bytes 393220
  58.3 10.5 %copy-start.4 = (bf16[256,256]{1,0:T(8,128)(2,1)S(1)}, bf16[256,256]{1,0:T(8,128)(2,1)}, u32[]{:S(2)}) copy-start(bf16[256,256]{1,0:T(8,128)(2,1)} %param.26) | copy-start | bytes 393220
  527.7 36.5 %copy-start.5 = (bf16[256,256]{1,0:T(8,128)(2,1)S(1)}, bf16[256,256]{1,0:T(8,128)(2,1)}, u32[]{:S(2)}) copy-start(bf16[256,256]{1,0:T(8,128)(2,1)} %param.27) | copy-start | bytes 393220
  564.3 1.4 copy-start.1
Sparse Core Ops, SparseCore 0:
  68.6 302.9 all-gather.1
where the time goes:
time: 574 us; the launch traced here: 572 us
  waiting for transfers between devices  302 us (53%)
  blocking collectives  114 us (20%)
  matrix products  82.4 us (14%)
  local copies, waits for them, and re-layouts  39.6 us (7%)
  between operations  14.3 us (2%)
  other arithmetic  10.6 us (2%)
  starting transfers between devices  8.41 us (1%)
    all_gather x1, waiting for transfers between devices, shards(): all_keys = lax.all_gather(local_keys, ('grp', 'dom'), axis=0, tiled=True)  302 us
    psum x1, blocking collectives, shards(): total_sums = lax.psum(own_sums, ('grp', 'dom')).astype(jnp.bfloat16)  114 us
    dot_general x16, matrix products, partial_one_block(): lax.dot_general(kernel, value, (((0,), (0,)), ((), ())), preferred_elemen...  41.7 us
    dot_general x16, matrix products, apply_one_block(): jnp.dot(kernel, block_sums, preferred_element_type=jnp.float32)  35.7 us
    gather x1, local copies, waits for them, and re-layouts, shards(): preact = target[:, None, :] + source[neighbours] + edge_bias  31.6 us
  transfers between devices with their start and end apart: 3, of which 1 were waited for; matrix products, arithmetic and copies ran while one was open for 1% of the time, Pallas kernels for 0%

commit v1 on v0

v1 whole, which is shorter than its diff:
```python
import functools
import math

import jax
import jax.numpy as jnp
from jax import lax
from jax.experimental import pallas as pl
from jax.experimental.pallas import tpu as pltpu
from jax.sharding import PartitionSpec as P

bf16 = jnp.bfloat16
f32 = jnp.float32
MESH = pl.DeviceIdType.MESH
AXES = ("grp", "dom")
VM = pl.BlockSpec(memory_space=pltpu.VMEM)


def dotf(a, b):
    return jnp.dot(a, b, preferred_element_type=f32)


def dot_nt(a, b):
    return lax.dot_general(a, b, (((1,), (1,)), ((), ())), preferred_element_type=f32)


def dot_tn(a, b):
    return lax.dot_general(a, b, (((0,), (0,)), ((), ())), preferred_element_type=f32)


def rows_at(start, size):
    return pl.ds(pl.multiple_of(start, size), size)


def gelu(x):
    return 0.5 * x * (1.0 + jnp.tanh(math.sqrt(2.0 / math.pi) * (x + 0.044715 * (x * x * x))))


def pick_rows(ids, table):
    rows = table.shape[0]
    count = ids.shape[1]
    chosen = lax.broadcasted_iota(jnp.int32, (rows, count), 0) == ids
    return dot_tn(chosen.astype(f32).astype(bf16), table).astype(bf16)


def enter(partners):
    barrier = pltpu.get_barrier_semaphore()
    for device in partners:
        pl.semaphore_signal(barrier, inc=1, device_id=device, device_id_type=MESH)
    pl.semaphore_wait(barrier, len(partners))


def halo_kernel(groups, doms, nodes, send_rows, halo, outgoing, landing, send_sem, recv_sem):
    count = groups * doms
    me = lax.axis_index("grp") * doms + lax.axis_index("dom")
    before = (me + count - 1) % count
    after = (me + 1) % count
    prev = (before // doms, before % doms)
    nxt = (after // doms, after % doms)
    half = halo.shape[0] // 2
    outgoing[...] = pick_rows(send_rows[...], nodes[...])
    enter((prev, nxt))
    to_prev = pltpu.make_async_remote_copy(
        src_ref=outgoing.at[:half],
        dst_ref=landing.at[half:],
        send_sem=send_sem.at[0],
        recv_sem=recv_sem.at[0],
        device_id=prev,
        device_id_type=MESH,
    )
    to_next = pltpu.make_async_remote_copy(
        src_ref=outgoing.at[half:],
        dst_ref=landing.at[:half],
        send_sem=send_sem.at[1],
        recv_sem=recv_sem.at[1],
        device_id=nxt,
        device_id_type=MESH,
    )
    to_prev.start()
    to_next.start()
    to_prev.wait()
    to_next.wait()
    halo[...] = landing[...]


def halo_rows(groups, doms, nodes, send_rows):
    count = send_rows.shape[0]
    shape = (count, nodes.shape[1])
    return pl.pallas_call(
        functools.partial(halo_kernel, groups, doms),
        out_shape=jax.ShapeDtypeStruct(shape, bf16),
        in_specs=[VM, VM],
        out_specs=VM,
        scratch_shapes=[
            pltpu.VMEM(shape, bf16),
            pltpu.VMEM(shape, bf16),
            pltpu.SemaphoreType.DMA((2,)),
            pltpu.SemaphoreType.DMA((2,)),
        ],
        compiler_params=pltpu.CompilerParams(collective_id=0, has_side_effects=True),
        name="halo",
    )(nodes, send_rows.reshape(1, count))


def front_kernel(
    nodes, halo, nbr, ids, w_dst, w_src, w_msg, bias, w_query, w_key, w_value,
    updated, query, value, keys, source, target, onehot, messages, normed,
):
    rows, channels = nodes.shape
    total = source.shape[0]
    slots = nbr.shape[1]
    block = onehot.shape[0] // slots
    source[:rows, :] = dotf(nodes[...], w_src[...]).astype(bf16)
    source[rows:, :] = dotf(halo[...], w_src[...]).astype(bf16)
    target[...] = dotf(nodes[...], w_dst[...]) + bias[...]

    def body(step, carry):
        here = rows_at(step * block, block)
        index = nbr[here, :]
        lane = lax.broadcasted_iota(jnp.int32, (block, total), 1).astype(jnp.int16)
        for k in range(slots):
            column = jnp.broadcast_to(index[:, k : k + 1], (block, total)).astype(jnp.int16)
            onehot[k * block : (k + 1) * block, :] = jnp.where(
                column == lane, jnp.ones((), bf16), jnp.zeros((), bf16)
            )
        picked = dotf(onehot[...], source[...])
        base = target[here, :]
        total_gelu = jnp.zeros((block, channels), f32)
        for k in range(slots):
            total_gelu = total_gelu + gelu(picked[k * block : (k + 1) * block] + base)
        messages[here, :] = (total_gelu * (1.0 / slots)).astype(bf16)
        return carry

    lax.fori_loop(0, rows // block, body, 0)
    new = (nodes[...].astype(f32) + dotf(messages[...], w_msg[...])).astype(bf16)
    updated[...] = new
    wide = new.astype(f32)
    unit = (wide * lax.rsqrt(jnp.mean(wide * wide, axis=-1, keepdims=True) + 1e-6)).astype(bf16)
    normed[...] = unit
    query[...] = dotf(unit, w_query[...]).astype(bf16)
    value[...] = dotf(unit, w_value[...]).astype(bf16)
    keys[...] = dotf(pick_rows(ids[...], normed[...]), w_key[...]).astype(bf16)


def front(nodes, halo, nbr, ids, w_dst, w_src, w_msg, bias, w_query, w_key, w_value):
    rows, channels = nodes.shape
    total = rows + halo.shape[0]
    count = ids.shape[0]
    slots = nbr.shape[1]
    block = math.gcd(rows, 128)
    full = jax.ShapeDtypeStruct((rows, channels), bf16)
    return pl.pallas_call(
        front_kernel,
        out_shape=(full, full, full, jax.ShapeDtypeStruct((count, channels), bf16)),
        in_specs=[VM] * 11,
        out_specs=(VM,) * 4,
        scratch_shapes=[
            pltpu.VMEM((total, channels), bf16),
            pltpu.VMEM((rows, channels), f32),
            pltpu.VMEM((slots * block, total), bf16),
            pltpu.VMEM((rows, channels), bf16),
            pltpu.VMEM((rows, channels), bf16),
        ],
        compiler_params=pltpu.CompilerParams(vmem_limit_bytes=24 << 20),
        name="front",
    )(
        nodes, halo, nbr, ids.reshape(1, count), w_dst, w_src, w_msg,
        bias.reshape(1, channels), w_query, w_key, w_value,
    )


RING = 4
LOG2E = math.log2(math.e)


def smooth_kernel(
    query, value, keys, smooth,
    all_query, all_value, all_keys, kernel, part, own, sums,
    relay, slabs, mid, low, small, accum, landing, send_sem, recv_sem,
):
    rows, channels = query.shape
    block = keys.shape[0]
    quad, slab = RING * block, RING * RING * block
    half = slab // 2
    chunk = quad

    grp, dom = lax.axis_index("grp"), lax.axis_index("dom")
    core, x = grp % 2, (grp // 2) * 2 + dom % 2
    y, z = (dom // 2) % RING, dom // (2 * RING)
    inner = y * (1 - core) + z * core
    outer = z * (1 - core) + y * core

    def device(i, m, o, c):
        yy = i * (1 - core) + o * core
        zz = o * (1 - core) + i * core
        return ((m // 2) * 2 + c, zz * (2 * RING) + yy * 2 + m % 2)

    def turn(a, d):
        return (a + d) % RING

    inner_peer = {d: device(turn(inner, d), x, outer, core) for d in (1, 2, 3)}
    mid_peer = {d: device(inner, turn(x, d), outer, core) for d in (1, 2, 3)}
    right = device(inner, x, turn(outer, 1), core)
    left = device(inner, x, turn(outer, 3), core)
    other = device(inner, x, outer, 1 - core)
    enter((*inner_peer.values(), *mid_peer.values(), right, left, other))

    used = [0]

    def push(src, dst, where):
        n = used[0]
        used[0] += 1
        copy = pltpu.make_async_remote_copy(
            src_ref=src,
            dst_ref=dst,
            send_sem=send_sem.at[n],
            recv_sem=recv_sem.at[n],
            device_id=where,
            device_id_type=MESH,
        )
        copy.start()
        return copy

    pending = []

    def arrive(copies):
        for copy in copies:
            copy.wait_recv()
            pending.append(copy)

    def slab_at(d):
        return turn(outer, d) * slab

    me_block = (outer * RING * RING + x * RING + inner) * block
    me_quad = (outer * RING + x) * quad

    def gather(first, table, work):
        table[rows_at(me_block, block), :] = first[...]
        arrive([push(first, table.at[rows_at(me_block, block)], inner_peer[d]) for d in (2, 1, 3)])
        here = table.at[rows_at(me_quad, quad)]
        arrive([push(here, here, mid_peer[d]) for d in (2, 1, 3)])
        here = table.at[rows_at(slab_at(0), slab)]
        to_right = push(here, here, right)
        to_left = push(here, here, left)
        work(0)
        arrive([to_right])
        top = table.at[rows_at(slab_at(3), half)]
        far_right = push(top, top, right)
        arrive([to_left])
        bottom = table.at[rows_at(slab_at(1) + half, half)]
        far_left = push(bottom, bottom, left)
        work(3)
        work(1)
        arrive([far_right, far_left])
        work(2)

    all_query[:rows, :] = query[...]
    all_value[:rows, :] = value[...]
    swap_query = push(query, all_query.at[rows:], other)
    swap_value = push(value, all_value.at[rows:], other)

    def kernel_rows(d):
        if d == 0:
            arrive([swap_query])

        def body(step, carry):
            here = rows_at(slab_at(d) + step * chunk, chunk)
            dots = dot_nt(all_keys[here, :], all_query[...])
            kernel[here, :] = jnp.exp2(dots * (2.0 * channels**-0.5 * LOG2E)).astype(bf16)
            return carry

        lax.fori_loop(0, slab // chunk, body, 0)

    gather(keys, all_keys, kernel_rows)
    arrive([swap_value])

    def partial(d, second, extra=None):
        start = slab_at(d) + second * half

        def body(step, carry):
            here = rows_at(start + step * chunk, chunk)
            value_here = dotf(kernel[here, :], all_value[...])
            if extra is not None:
                value_here = value_here + extra[rows_at(step * chunk, chunk), :].astype(f32)
            part[here, :] = value_here.astype(bf16)
            return carry

        lax.fori_loop(0, half // chunk, body, 0)
        return part.at[rows_at(start, half)]

    relay_right = push(partial(2, 0), relay.at[0], right)
    relay_left = push(partial(2, 1), relay.at[1], left)
    right_low = push(partial(1, 1), slabs.at[0, half:], right)
    left_high = push(partial(3, 0), slabs.at[1, :half], left)

    def own_rows(step, carry):
        here = rows_at(slab_at(0) + step * chunk, chunk)
        own[rows_at(step * chunk, chunk), :] = dotf(kernel[here, :], all_value[...])
        return carry

    lax.fori_loop(0, slab // chunk, own_rows, 0)
    arrive([relay_right])
    right_high = push(partial(1, 0, relay.at[0]), slabs.at[0, :half], right)
    arrive([relay_left])
    left_low = push(partial(3, 1, relay.at[1]), slabs.at[1, half:], left)
    arrive([right_low, left_high, right_high, left_low])

    def add_slabs(step, carry):
        here = rows_at(step * chunk, chunk)
        both = slabs[0, here, :].astype(f32) + slabs[1, here, :].astype(f32)
        whole = own[here, :] + both
        own[here, :] = whole
        mid[here, :] = whole.astype(bf16)
        return carry

    lax.fori_loop(0, slab // chunk, add_slabs, 0)
    mid_copies = [
        push(mid.at[rows_at(turn(x, d) * quad, quad)], slabs.at[2, (d - 1) * quad : d * quad], mid_peer[d])
        for d in (2, 1, 3)
    ]
    arrive(mid_copies)
    four = own[rows_at(x * quad, quad), :]
    for d in range(3):
        four = four + slabs[2, d * quad : (d + 1) * quad, :].astype(f32)
    own[:quad, :] = four
    low[...] = four.astype(bf16)
    low_copies = [
        push(low.at[rows_at(turn(inner, d) * block, block)], small.at[d - 1], inner_peer[d])
        for d in (2, 1, 3)
    ]
    arrive(low_copies)
    one = own[rows_at(inner * block, block), :]
    for d in range(3):
        one = one + small[d].astype(f32)
    small[3] = one.astype(bf16)

    tile = rows // 2

    def apply(d):
        def body(step, carry):
            here = rows_at((2 * rows // tile - 1 - step) * tile, tile)
            added = dot_tn(
                kernel[rows_at(slab_at(d), slab), here], sums[rows_at(slab_at(d), slab), :]
            )
            accum[here, :] = added if d == 0 else accum[here, :] + added
            return carry

        if d != 2:
            lax.fori_loop(0, 2 * rows // tile, body, 0)
            return
        lax.fori_loop(0, rows // tile, body, 0)
        swap = push(accum.at[rows:], landing, other)
        lax.fori_loop(rows // tile, 2 * rows // tile, body, 0)
        arrive([swap])

    gather(small.at[3], sums, apply)
    smooth[...] = accum[:rows, :] + landing[...]
    for copy in pending:
        copy.wait_send()


def smooth_rows(query, value, keys):
    rows, channels = query.shape
    block = keys.shape[0]
    marks = RING**3 * block
    slab = RING * RING * block
    copies = 2 * 10 + 2 + 6 + 6 + 1
    return pl.pallas_call(
        smooth_kernel,
        out_shape=jax.ShapeDtypeStruct((rows, channels), f32),
        in_specs=[VM] * 3,
        out_specs=VM,
        scratch_shapes=[
            pltpu.VMEM((2 * rows, channels), bf16),
            pltpu.VMEM((2 * rows, channels), bf16),
            pltpu.VMEM((marks, channels), bf16),
            pltpu.VMEM((marks, 2 * rows), bf16),
            pltpu.VMEM((marks, channels), bf16),
            pltpu.VMEM((slab, channels), f32),
            pltpu.VMEM((marks, channels), bf16),
            pltpu.VMEM((2, slab // 2, channels), bf16),
            pltpu.VMEM((3, slab, channels), bf16),
            pltpu.VMEM((slab, channels), bf16),
            pltpu.VMEM((RING * block, channels), bf16),
            pltpu.VMEM((RING, block, channels), bf16),
            pltpu.VMEM((2 * rows, channels), f32),
            pltpu.VMEM((rows, channels), f32),
            pltpu.SemaphoreType.DMA((copies,)),
            pltpu.SemaphoreType.DMA((copies,)),
        ],
        compiler_params=pltpu.CompilerParams(
            collective_id=1, has_side_effects=True, vmem_limit_bytes=44 << 20
        ),
        name="smooth",
    )(query, value, keys)


def finish_kernel(smooth, updated, w_out, result, term):
    wide = smooth[...]
    scaled = wide * lax.rsqrt(jnp.mean(wide * wide, axis=-1, keepdims=True) + 1e-6)
    term[...] = scaled
    result[...] = (updated[...].astype(f32) + dotf(scaled.astype(bf16), w_out[...])).astype(bf16)


def finish(smooth, updated, w_out):
    rows, channels = smooth.shape
    block = rows // 4
    tile = pl.BlockSpec((block, channels), lambda i: (i, 0))
    return pl.pallas_call(
        finish_kernel,
        out_shape=(
            jax.ShapeDtypeStruct((rows, channels), bf16),
            jax.ShapeDtypeStruct((rows, channels), f32),
        ),
        grid=(rows // block,),
        in_specs=[tile, tile, pl.BlockSpec((channels, channels), lambda i: (0, 0))],
        out_specs=(tile, tile),
        name="finish",
    )(smooth, updated, w_out)


def shards(
    groups, doms,
    nodes, neighbours, send_rows, landmark_ids,
    w_dst, w_src, w_msg, edge_bias, w_query, w_key, w_value, w_out,
):
    halo = halo_rows(groups, doms, nodes, send_rows)
    updated, query, value, keys = front(
        nodes, halo, neighbours, landmark_ids, w_dst, w_src, w_msg, edge_bias, w_query, w_key, w_value
    )
    smooth = smooth_rows(query, value, keys)
    return finish(smooth, updated, w_out)


def solution(mesh):
    groups, doms = mesh.shape["grp"], mesh.shape["dom"]
    split, line, whole = P(AXES, None), P(AXES), P()
    return jax.shard_map(
        functools.partial(shards, groups, doms),
        mesh=mesh,
        in_specs=(split, split, line, line) + (whole,) * 8,
        out_specs=(split, split),
        check_vma=False,
    )
```

time: 574 us -> 116 us (0.20)
  waiting for transfers between devices: 302 us -> 0 us
  blocking collectives: 114 us -> 0 us
  Pallas kernels: 0 us -> 109 us
  matrix products: 82.4 us -> 0 us
  local copies, waits for them, and re-layouts: 39.6 us -> 4.67 us
  between operations: 14.3 us -> 0.81 us
  other arithmetic: 10.6 us -> 0 us
  starting transfers between devices: 8.41 us -> 0 us
    all_gather x1 -> x0, waiting for transfers between devices: 302 us -> none  [shards(): all_keys = lax.all_gather(local_keys, ('grp', 'dom'), axis=0, tiled=True)]
    psum x1 -> x0, blocking collectives: 114 us -> none  [shards(): total_sums = lax.psum(own_sums, ('grp', 'dom')).astype(jnp.bfloat16)]
    pallas_call x0 -> x4, Pallas kernels: none -> 109 us  [the longest x1 81.6 us: smooth_rows(): pl.pallas_call(smooth_kernel, out_shape=jax.ShapeDtypeStruct((rows, chann...]
    dot_general x39 -> x0, matrix products: 82.4 us -> none  [the longest x16 41.7 us: partial_one_block(): lax.dot_general(kernel, value, (((0,), (0,)), ((), ())), preferred_elemen...]
    gather x4 -> x0, local copies, waits for them, and re-layouts: 36 us -> none  [the longest x1 31.6 us: shards(): preact = target[:, None, :] + source[neighbours] + edge_bias]
    ppermute x2 -> x0, starting transfers between devices: 8.37 us -> none  [the longest x1 6.72 us: extended_2(): lax.ppermute(head, axis, [((i + 1) % count, i) for i in range(count)])]
    reduce_sum x2 -> x0, other arithmetic: 8.05 us -> none  [the longest x1 7.84 us: shards(): messages = jnp.mean(jax.nn.gelu(preact), axis=1).astype(jnp.bfloat16)]
  transfers between devices with their start and end apart: 3 -> 0, of which waited for: 1 -> 0; matrix products, arithmetic and copies ran while one was open for 1% -> 0% of each run, Pallas kernels for 0% -> 0%
where the time goes in v1:
time: 116 us; the launch traced here: 114 us
  Pallas kernels  109 us (94%)
  local copies, waits for them, and re-layouts  4.67 us (4%)
    pallas_call x1, Pallas kernels, smooth_rows(): pl.pallas_call(smooth_kernel, out_shape=jax.ShapeDtypeStruct((rows, chann...  81.6 us
    pallas_call x1, Pallas kernels, halo_rows(): pl.pallas_call(functools.partial(halo_kernel, groups, doms), out_shape=ja...  13.3 us
    pallas_call x1, Pallas kernels, front(): pl.pallas_call(front_kernel, out_shape=(full, full, full, jax.ShapeDtypeS...  9.91 us
    unnamed x25, local copies, waits for them, and re-layouts  4.67 us
    pallas_call x1, Pallas kernels, finish(): pl.pallas_call(finish_kernel, out_shape=(jax.ShapeDtypeStruct((rows, chan...  3.88 us

profile of v1, /device:TPU:0, one launch (start us, length us, event | category | flops | bytes accessed | tf_op | source)
XLA Modules:
  0.0 114.2 jit_solution(11770517438259273861)
XLA Ops:
  0.6 0.0 copy-start.1
  0.6 0.0 copy-start.7
  0.6 13.3 %halo.1 = bf16[256,256]{1,0:T(8,128)(2,1)} custom-call(bf16[1024,256]{1,0:T(8,128)(2,1)} %nodes.3, s32[1,256]{1,0:T(1,128)} %bitcast.5), custom_call_target="tpu_custom_call" | custom-call | tf_op jit(solution)/shard_map/halo/pallas_call | solution.py:88
  14.0 0.0 copy-start.2
  14.0 0.0 copy-start.4
  14.0 0.0 copy-start.5
  14.0 0.0 copy-start.6
  14.0 0.0 copy-start.10
  14.0 0.0 copy-start.11
  14.1 1.1 copy.14.nbr
  15.1 0.0 copy-done.1
  15.1 0.0 copy-done.7
  15.1 0.0 copy-done.2
  15.1 0.0 copy-done.4
  15.2 0.0 copy-done.5
  15.2 0.0 copy-done.6
  15.2 0.0 copy-done.10
  15.2 0.0 copy-done.11
  15.2 0.0 copy-start.8
  15.2 0.9 copy-done.8
  16.1 0.0 copy-start.9
  16.1 0.9 copy-done.9
  17.0 9.9 %front.1 = (bf16[1024,256]{1,0:T(8,128)(2,1)S(1)}, bf16[1024,256]{1,0:T(8,128)(2,1)S(1)}, bf16[1024,256]{1,0:T(8,128)(2,1)S(1)}, bf16[64,256]{1,0:T(8,128)(2,1)S(1)}) custom-call(bf16[1024,256]{1,0:T(8,128)(2,1)S(1)} %copy-done.1, bf16[256,256]{1,0:T(8,128)(2,1)S(1)} %copy-done.2, s32[1024,8]{1,0:T(8,128)S(1)} %copy.14.nbr, s32[1,64]{1,0:T(1,128)S(1)} %bitcast.4, ...), custom_call_target="tpu_custom_call" | custom-call | tf_op jit(solution)/shard_map/front/pallas_call | solution.py:151
  26.9 0.0 copy-start.3
  26.9 0.8 copy-done.3
  27.7 81.6 %smooth.1 = f32[1024,256]{1,0:T(8,128)S(1)} custom-call(bf16[1024,256]{1,0:T(8,128)(2,1)S(1)} %get-tuple-element.6.query, bf16[1024,256]{1,0:T(8,128)(2,1)S(1)} %get-tuple-element.7.value, bf16[64,256]{1,0:T(8,128)(2,1)S(1)} %get-tuple-element.8.keys), custom_call_target="tpu_custom_call" | custom-call | tf_op jit(solution)/shard_map/smooth/pallas_call | solution.py:367
  109.3 0.0 copy-start
  109.3 1.0 copy-done
  110.3 3.9 %finish.1 = (bf16[1024,256]{1,0:T(8,128)(2,1)}, f32[1024,256]{1,0:T(8,128)}) custom-call(f32[1024,256]{1,0:T(8,128)} %copy-done, bf16[1024,256]{1,0:T(8,128)(2,1)} %copy-done.3, bf16[256,256]{1,0:T(8,128)(2,1)} %w_out.1), custom_call_target="tpu_custom_call" | custom-call | tf_op jit(solution)/shard_map/finish/pallas_call | solution.py:408
Async XLA Ops:
  0.6 14.5 %copy-start.1 = (bf16[1024,256]{1,0:T(8,128)(2,1)S(1)}, bf16[1024,256]{1,0:T(8,128)(2,1)}, u32[]{:S(2)}) copy-start(bf16[1024,256]{1,0:T(8,128)(2,1)} %nodes.3) | copy-start | bytes 1572868
  0.6 14.5 %copy-start.7 = (bf16[256,256]{1,0:T(8,128)(2,1)S(1)}, bf16[256,256]{1,0:T(8,128)(2,1)}, u32[]{:S(2)}) copy-start(bf16[256,256]{1,0:T(8,128)(2,1)} %w_query.1) | copy-start | bytes 393220
  14.0 1.2 %copy-start.2 = (bf16[256,256]{1,0:T(8,128)(2,1)S(1)}, bf16[256,256]{1,0:T(8,128)(2,1)}, u32[]{:S(2)}) copy-start(bf16[256,256]{1,0:T(8,128)(2,1)} %halo.1) | copy-start | bytes 393220
  14.0 1.2 %copy-start.4 = (bf16[256,256]{1,0:T(8,128)(2,1)S(1)}, bf16[256,256]{1,0:T(8,128)(2,1)}, u32[]{:S(2)}) copy-start(bf16[256,256]{1,0:T(8,128)(2,1)} %w_dst.1) | copy-start | bytes 393220
  14.0 1.2 %copy-start.5 = (bf16[256,256]{1,0:T(8,128)(2,1)S(1)}, bf16[256,256]{1,0:T(8,128)(2,1)}, u32[]{:S(2)}) copy-start(bf16[256,256]{1,0:T(8,128)(2,1)} %w_src.1) | copy-start | bytes 393220
  14.0 1.1 %copy-start.6 = (bf16[256,256]{1,0:T(8,128)(2,1)S(1)}, bf16[256,256]{1,0:T(8,128)(2,1)}, u32[]{:S(2)}) copy-start(bf16[256,256]{1,0:T(8,128)(2,1)} %w_msg.1) | copy-start | bytes 393220
  14.0 1.1 %copy-start.10 = (f32[256]{0:T(256)S(1)}, f32[256]{0:T(256)}, u32[]{:S(2)}) copy-start(f32[256]{0:T(256)} %param.19) | copy-start | bytes 3076
  14.0 1.1 %copy-start.11 = (s32[64]{0:T(128)S(1)}, s32[64]{0:T(128)}, u32[]{:S(2)}) copy-start(s32[64]{0:T(128)} %param.15) | copy-start | bytes 772
  15.2 0.9 copy-start.8
  16.1 0.9 copy-start.9
  26.9 0.8 copy-start.3
  109.3 1.0 copy-start
